TPU v7x, 32 devices: a whole 2x2x4 slice. The times are simulated.
32 devices in a mesh: row: 8 (over y, x, core), col: 4 (over z).
Axes of the slice: x: 2, y: 2, z: 4, core: 2. Of those that a mesh axis runs over, the one named last changes fastest.
Arguments:
- trailing: float32 [6144, 4096], P('row', 'col'), may hold values from -6 to 6
- column_block: bfloat16 [6144, 1024], P('row', 'col'), may hold values from -6 to 6
- row_block: bfloat16 [1024, 4096], P('row', 'col'), may hold values from -0.1875 to 0.1875
- lower_inv: bfloat16 [1024, 1024], replicated, may hold values from -1 to 1, as said below
- upper_inv: bfloat16 [1024, 1024], replicated, may hold values from -2 to 2, as said below
Outputs:
- lower_panel: bfloat16 [6144, 1024], P('row', 'col')
- upper_panel: bfloat16 [1024, 4096], P('row', 'col')
- updated: float32 [6144, 4096], P('row', 'col')
Inputs may be any that keep to these rules, and one draw needn't show every extreme that they name: `lower_inv`: lower triangular with ones on the diagonal. `upper_inv`: upper triangular with diagonal entries between 0.5 and 2.
All inputs are finite; a program needn't handle non-finite values.
Results may differ from a plain program's by a relative error of at most 0.0044.
Values may be sent and summed in bfloat16 or wider, within the bound.
A program may use at most 64 MiB of HBM per device.

v0:
```python
import jax
import jax.numpy as jnp
from jax import lax
from jax.sharding import PartitionSpec as P


def on_device(trailing, column_block, row_block, lower_inv, upper_inv):
    col_share = column_block.shape[1]
    row_share = row_block.shape[0]
    col_start = lax.axis_index("col") * col_share
    row_start = lax.axis_index("row") * row_share
    factor = upper_inv
    lower_full = jnp.dot(
        lax.all_gather(column_block, "col", axis=1, tiled=True),
        factor,
        preferred_element_type=jnp.float32,
    ).astype(jnp.bfloat16)
    factor = lower_inv
    upper_full = jnp.dot(
        factor,
        lax.all_gather(row_block, "row", axis=0, tiled=True),
        preferred_element_type=jnp.float32,
    ).astype(jnp.bfloat16)
    product = jnp.dot(lower_full, upper_full, preferred_element_type=jnp.float32)
    lower_tile = lax.dynamic_slice_in_dim(lower_full, col_start, col_share, 1)
    upper_tile = lax.dynamic_slice_in_dim(upper_full, row_start, row_share, 0)
    updated = trailing - product
    return (lower_tile, upper_tile, updated)


def solution(mesh):
    in_specs = (P("row", "col"), P("row", "col"), P("row", "col"), P(), P())
    out_specs = (P("row", "col"), P("row", "col"), P("row", "col"))
    return jax.shard_map(
        on_device, mesh=mesh, in_specs=in_specs, out_specs=out_specs, check_vma=False
    )
```

profile of v0, /device:TPU:0, one launch (start us, length us, event | category | flops | bytes accessed | tf_op | source)
XLA Modules:
  0.0 93.0 jit_solution(8704201044639735974)
XLA Ops:
  7.2 0.0 copy-start
  7.2 0.0 all-gather.3.cloned.1.call-start
  7.2 0.7 all-gather.3.cloned.1.call-update
  7.9 0.0 all-gather.5.cloned.1.call-start
  8.0 0.7 all-gather.5.cloned.1.call-update
  8.7 41.3 %all-gather.3.cloned.1.call-done = bf16[768,1024]{1,0:T(8,128)(2,1)} async-done(((bf16[768,256]{1,0:T(8,128)(2,1)}), bf16[768,1024]{1,0:T(8,128)(2,1)}) %all-gather.3.cloned.1.call-update) | async-done | bytes 1572880 | tf_op jit(solution)/shard_map/all_gather | solution.py:14
  50.0 3.9 %convolution_convert_fusion.1 = bf16[768,1024]{1,0:T(8,128)(2,1)S(1)} fusion(bf16[768,1024]{1,0:T(8,128)(2,1)} %all-gather.3.cloned.1.call-done, bf16[1024,1024]{1,0:T(8,128)(2,1)} %param.9), kind=kOutput, calls=%fused_computation.2 | convolution fusion | flops 1611399168 | bytes 5242880 | tf_op jit(solution)/shard_map/dot_general | solution.py:13
  53.9 0.0 copy-start.1
  53.9 1.1 %copy-done.1 = bf16[768,1024]{1,0:T(8,128)(2,1)} copy-done((bf16[768,1024]{1,0:T(8,128)(2,1)}, bf16[768,1024]{1,0:T(8,128)(2,1)S(1)}, u32[]{:S(2)}) %copy-start.1) | copy-done | bytes 1572888
  55.0 0.8 constant_dynamic-slice_fusion.1
  55.8 22.1 %all-gather.5.cloned.1.call-done = bf16[1024,1024]{1,0:T(8,128)(2,1)} async-done(((bf16[128,1024]{1,0:T(8,128)(2,1)}), bf16[1024,1024]{1,0:T(8,128)(2,1)}) %all-gather.5.cloned.1.call-update) | async-done | bytes 2097168 | tf_op jit(solution)/shard_map/all_gather | solution.py:21
  77.9 0.0 copy-done
  77.9 0.0 copy-start.2
  77.9 0.0 copy-start.3
  77.9 4.1 %convolution_convert_fusion = bf16[1024,1024]{1,0:T(8,128)(2,1)S(1)} fusion(bf16[1024,1024]{1,0:T(8,128)(2,1)S(1)} %copy-done, bf16[1024,1024]{1,0:T(8,128)(2,1)} %all-gather.5.cloned.1.call-done), kind=kOutput, calls=%fused_computation | convolution fusion | flops 2148532224 | bytes 6291456 | tf_op jit(solution)/shard_map/dot_general | solution.py:19
  82.0 0.7 constant_dynamic-slice_fusion
  82.7 0.0 copy-done.2
  82.7 0.0 copy-done.3
  82.7 3.5 %convolution_subtract_fusion = f32[768,1024]{1,0:T(8,128)} fusion(f32[768,1024]{1,0:T(8,128)S(1)} %copy-done.3, bf16[768,1024]{1,0:T(8,128)(2,1)S(1)} %copy-done.2, bf16[1024,1024]{1,0:T(8,128)(2,1)S(1)} %convolution_convert_fusion), kind=kOutput, calls=%fused_computation.1 | convolution fusion | flops 1611399168 | bytes 9961472 | tf_op jit(solution)/shard_map/dot_general | solution.py:24
Async XLA Ops:
  7.2 70.8 %copy-start = (bf16[1024,1024]{1,0:T(8,128)(2,1)S(1)}, bf16[1024,1024]{1,0:T(8,128)(2,1)}, u32[]{:S(2)}) copy-start(bf16[1024,1024]{1,0:T(8,128)(2,1)} %param.8) | copy-start | bytes 6291460
  7.2 42.8 %all-gather.3.cloned.1.call-start = ((), (), s32[]{:S(2)}) async-start(), calls=%async_computation | async-start | bytes 1966080 | tf_op jit(solution)/shard_map/all_gather | solution.py:14
  7.9 70.0 %all-gather.5.cloned.1.call-start = ((), (), s32[]{:S(2)}) async-start(), calls=%async_computation.1 | async-start | bytes 2359296 | tf_op jit(solution)/shard_map/all_gather | solution.py:21
  53.9 1.1 %copy-start.1 = (bf16[768,1024]{1,0:T(8,128)(2,1)}, bf16[768,1024]{1,0:T(8,128)(2,1)S(1)}, u32[]{:S(2)}) copy-start(bf16[768,1024]{1,0:T(8,128)(2,1)S(1)} %convolution_convert_fusion.1) | copy-start | bytes 4718596
  77.9 4.8 %copy-start.2 = (bf16[768,1024]{1,0:T(8,128)(2,1)S(1)}, bf16[768,1024]{1,0:T(8,128)(2,1)}, u32[]{:S(2)}) copy-start(bf16[768,1024]{1,0:T(8,128)(2,1)} %copy-done.1) | copy-start | bytes 4718596
  77.9 4.8 %copy-start.3 = (f32[768,1024]{1,0:T(8,128)S(1)}, f32[768,1024]{1,0:T(8,128)}, u32[]{:S(2)}) copy-start(f32[768,1024]{1,0:T(8,128)} %param.5) | copy-start | bytes 9437188
Sparse Core Ops, SparseCore 0:
  9.5 40.3 all-gather.2
  51.9 25.9 all-gather.4
where the time goes:
time: 93.2 us; the launch traced here: 93 us
  waiting for transfers between devices  64.8 us (70%)
  between operations  14.1 us (15%)
  matrix products  11.4 us (12%)
  local copies, waits for them, and re-layouts  2.68 us (3%)
    all_gather x1, waiting for transfers between devices, on_device(): lax.all_gather(column_block, 'col', axis=1, tiled=True)  41.3 us
    all_gather x1, waiting for transfers between devices, on_device(): lax.all_gather(row_block, 'row', axis=0, tiled=True)  22.1 us
    dot_general x1, matrix products, on_device(): jnp.dot(factor, lax.all_gather(row_block, 'row', axis=0, tiled=True), pre...  4.06 us
    dot_general x1, matrix products, on_device(): jnp.dot(lax.all_gather(column_block, 'col', axis=1, tiled=True), factor,...  3.86 us
    dot_general x1, matrix products, on_device(): jnp.dot(lower_full, upper_full, preferred_element_type=jnp.float32)  3.47 us
  transfers between devices with their start and end apart: 2, of which 2 were waited for; matrix products, arithmetic and copies ran while one was open for 5% of the time, Pallas kernels for 0%

commit v1 on v0

v1 whole, which is shorter than its diff:
```python
import functools

import jax
import jax.numpy as jnp
from jax import lax
from jax.experimental import pallas as pl
from jax.experimental.pallas import tpu as pltpu
from jax.sharding import PartitionSpec as P

MESH = pl.DeviceIdType.MESH
BLOCK = 256
COL_CHUNKS = 6
ROW_CHUNKS = 4
GROUPS = (2, 2, 1, 1)
AHEAD = 2


def reach(size, chunk):
    each = (size - 1) // 2
    extra = 1 if size % 2 == 0 else 0
    return (each + extra, each) if chunk % 2 == 0 else (each, each + extra)


def kernel(
    n_row, n_col,
    trailing, column_block, row_block, lower_inv, upper_inv,
    lower_tile, upper_tile, updated,
    gathered, strips, linv, uinv, lower, upper,
    local_sem, own_sem, col_send, col_recv, row_send, row_recv, sib_send, sib_recv,
):
    rows, share = column_block.shape
    depth, cols = row_block.shape
    order = lower_inv.shape[0]
    tall, wide = rows // COL_CHUNKS, cols // ROW_CHUNKS
    row, col = lax.axis_index("row"), lax.axis_index("col")
    chips = n_row // 2
    half = chips // 2
    core = lax.rem(row, 2)

    def snake(place):
        return place + (place // half) * (chips + half - 1 - 2 * place)

    place = snake(row // 2)

    def chip_at(offset):
        return snake(lax.rem(place + chips + offset, chips))

    sibling = {"row": row + 1 - 2 * core}
    row_next = {"row": chip_at(1) * 2 + core}
    row_prev = {"row": chip_at(-1) * 2 + core}
    col_next = {"col": lax.rem(col + 1, n_col)}
    col_prev = {"col": lax.rem(col + n_col - 1, n_col)}

    load_l = pltpu.make_async_copy(lower_inv, linv, local_sem.at[0])
    load_u = pltpu.make_async_copy(upper_inv, uinv, local_sem.at[1])
    load_t = pltpu.make_async_copy(trailing, updated, local_sem.at[2])
    mine_c = pltpu.make_async_copy(column_block, gathered.at[col], own_sem.at[0])
    my_rows = pl.ds(pl.multiple_of(row * depth, depth), depth)
    mine_r = pltpu.make_async_copy(row_block, strips.at[my_rows], own_sem.at[1])

    barrier = pltpu.get_barrier_semaphore()
    for device in (col_next, col_prev, row_next, row_prev, sibling):
        pl.semaphore_signal(barrier, inc=1, device_id=device, device_id_type=MESH)
    mine_c.start()
    mine_r.start()
    load_l.start()
    load_u.start()
    pl.semaphore_wait(barrier, 5)

    sent = []

    def send(src, dst, send_sem, recv_sem, device):
        copy = pltpu.make_async_remote_copy(
            src_ref=src, dst_ref=dst, send_sem=send_sem, recv_sem=recv_sem,
            device_id=device, device_id_type=MESH,
        )
        copy.start()
        sent.append(copy)

    def arrived(dst, sem):
        pltpu.make_async_copy(dst, dst, sem).wait()

    def col_slot(offset, chunk):
        owner = lax.rem(col + n_col + offset, n_col)
        return gathered.at[owner, pl.ds(chunk * tall, tall)]

    def col_send_to(way, step, chunk, src):
        offset = (1 - step) if way == 0 else (step - 1)
        send(
            src, col_slot(offset, chunk),
            col_send.at[way, step - 1, chunk], col_recv.at[way, step - 1, chunk],
            col_next if way == 0 else col_prev,
        )

    def col_own(chunk):
        src = column_block.at[pl.ds(chunk * tall, tall)]
        for way in range(2):
            if reach(n_col, chunk)[way] >= 1:
                col_send_to(way, 1, chunk, src)

    def col_event(step, chunk):
        for way in range(2):
            limit = reach(n_col, chunk)[way]
            if step <= limit:
                slot = col_slot(-step if way == 0 else step, chunk)
                arrived(slot, col_recv.at[way, step - 1, chunk])
                if step < limit:
                    col_send_to(way, step + 1, chunk, slot)

    def strip(offset, lane, chunk):
        owner = chip_at(offset) * 2 + lane
        start = pl.multiple_of(owner * depth, depth)
        return strips.at[pl.ds(start, depth), pl.ds(chunk * wide, wide)]

    def row_send_to(way, step, chunk, src):
        offset = (1 - step) if way == 0 else (step - 1)
        send(
            src, strip(offset, core, chunk),
            row_send.at[way, step - 1, chunk], row_recv.at[way, step - 1, chunk],
            row_next if way == 0 else row_prev,
        )

    def share_strip(offset, chunk, src):
        at = offset + half
        send(
            src, strip(offset, core, chunk),
            sib_send.at[at, chunk], sib_recv.at[at, chunk], sibling,
        )

    shared = [[] for _ in range(ROW_CHUNKS)]

    def row_own(chunk):
        src = row_block.at[:, pl.ds(chunk * wide, wide)]
        for way in range(2):
            if reach(chips, chunk)[way] >= 1:
                row_send_to(way, 1, chunk, src)
        share_strip(0, chunk, src)
        shared[chunk].append(0)

    def row_event(step, chunk):
        for way in range(2):
            limit = reach(chips, chunk)[way]
            if step <= limit:
                offset = -step if way == 0 else step
                slot = strip(offset, core, chunk)
                arrived(slot, row_recv.at[way, step - 1, chunk])
                if step < limit:
                    row_send_to(way, step + 1, chunk, slot)
                share_strip(offset, chunk, slot)
                shared[chunk].append(offset)

    def row_shared(chunk):
        for offset in shared[chunk]:
            arrived(strip(offset, 1 - core, chunk), sib_recv.at[offset + half, chunk])

    def make_upper(chunk):
        at = pl.ds(chunk * wide, wide)
        for i in range(order // BLOCK):
            end = (i + 1) * BLOCK
            upper[pl.ds(i * BLOCK, BLOCK), at] = jnp.dot(
                linv[pl.ds(i * BLOCK, BLOCK), pl.ds(0, end)],
                strips[pl.ds(0, end), at],
                preferred_element_type=jnp.float32,
            ).astype(jnp.bfloat16)

    def make_lower(first, count):
        at = pl.ds(first * tall, count * tall)
        parts = [gathered[k, at] for k in range(n_col)]
        left = jnp.concatenate(parts, axis=1)
        for j in range(order // BLOCK):
            end = (j + 1) * BLOCK
            lower[at, pl.ds(j * BLOCK, BLOCK)] = jnp.dot(
                left[:, :end],
                uinv[pl.ds(0, end), pl.ds(j * BLOCK, BLOCK)],
                preferred_element_type=jnp.float32,
            ).astype(jnp.bfloat16)
        if share % 128 == 0:
            lower_tile[at] = lower[at, pl.ds(pl.multiple_of(col * share, share), share)]
        else:
            for k in range(n_col):
                @pl.when(col == k)
                def _():
                    lower_tile[at] = lower[at, pl.ds(k * share, share)]

    def subtract(first, count):
        at = pl.ds(first * tall, count * tall)

        @pl.loop(0, cols // BLOCK)
        def _(j):
            across = pl.ds(pl.multiple_of(j * BLOCK, BLOCK), BLOCK)
            updated[at, across] -= jnp.dot(
                lower[at], upper[:, across], preferred_element_type=jnp.float32
            )

    col_depth = max(max(reach(n_col, q)) for q in range(COL_CHUNKS))
    row_depth = max(max(reach(chips, r)) for r in range(ROW_CHUNKS))
    col_ticks = COL_CHUNKS + col_depth - 1
    row_ticks = ROW_CHUNKS + row_depth - 1
    groups, first = [], 0
    for count in GROUPS:
        groups.append((first, count))
        first += count
    for chunk in range(AHEAD):
        col_own(chunk)
        row_own(chunk)
    load_t.start()
    waiting, made_upper = list(groups), 0
    ready, uppers = [], list(range(ROW_CHUNKS))
    waited_inputs = False
    for tick in range(max(col_ticks, row_ticks + 2) + 1):
        for step in range(1, col_depth + 1):
            chunk = tick - (step - 1)
            if 0 <= chunk < COL_CHUNKS:
                col_event(step, chunk)
        for step in range(1, row_depth + 1):
            chunk = tick - (step - 1)
            if 0 <= chunk < ROW_CHUNKS:
                row_event(step, chunk)
        if AHEAD + tick < COL_CHUNKS:
            col_own(AHEAD + tick)
        if AHEAD + tick < ROW_CHUNKS:
            row_own(AHEAD + tick)
        if tick == 0:
            mine_c.wait()
            mine_r.wait()
            load_l.wait()
            load_u.wait()
        chunk = tick - row_depth
        if 0 <= chunk < ROW_CHUNKS:
            row_shared(chunk)
            make_upper(chunk)
            uppers.remove(chunk)
            if not uppers:
                upper_tile[...] = upper[my_rows]
                load_t.wait()
        while waiting and sum(waiting[0]) - 1 + col_depth - 1 <= tick:
            make_lower(*waiting[0])
            ready.append(waiting.pop(0))
        if not uppers:
            while ready:
                subtract(*ready.pop(0))
    assert not waiting and not ready and not uppers
    for copy in sent:
        copy.wait_send()


def on_device(n_row, n_col, trailing, column_block, row_block, lower_inv, upper_inv):
    rows, share = column_block.shape
    depth, cols = row_block.shape
    order = lower_inv.shape[0]
    chips = n_row // 2
    steps, hops = n_col // 2, chips // 2
    narrow = jnp.bfloat16
    anywhere = pl.BlockSpec(memory_space=pltpu.HBM)
    inside = pl.BlockSpec(memory_space=pltpu.VMEM)
    dma = pltpu.SemaphoreType.DMA
    return pl.pallas_call(
        functools.partial(kernel, n_row, n_col),
        out_shape=(
            jax.ShapeDtypeStruct((rows, share), narrow),
            jax.ShapeDtypeStruct((depth, cols), narrow),
            jax.ShapeDtypeStruct((rows, cols), jnp.float32),
        ),
        in_specs=[anywhere] * 5,
        out_specs=(inside,) * 3,
        scratch_shapes=[
            pltpu.VMEM((n_col, rows, share), narrow),
            pltpu.VMEM((order, cols), narrow),
            pltpu.VMEM((order, order), narrow),
            pltpu.VMEM((order, order), narrow),
            pltpu.VMEM((rows, order), narrow),
            pltpu.VMEM((order, cols), narrow),
            dma((3,)),
            dma((2,)),
            dma((2, steps, COL_CHUNKS)),
            dma((2, steps, COL_CHUNKS)),
            dma((2, hops, ROW_CHUNKS)),
            dma((2, hops, ROW_CHUNKS)),
            dma((2 * hops + 1, ROW_CHUNKS)),
            dma((2 * hops + 1, ROW_CHUNKS)),
        ],
        compiler_params=pltpu.CompilerParams(
            collective_id=0, has_side_effects=True, vmem_limit_bytes=32 << 20
        ),
    )(trailing, column_block, row_block, lower_inv, upper_inv)


def solution(mesh):
    specs = P("row", "col")
    return jax.shard_map(
        functools.partial(on_device, mesh.shape["row"], mesh.shape["col"]),
        mesh=mesh,
        in_specs=(specs, specs, specs, P(), P()),
        out_specs=(specs,) * 3,
        check_vma=False,
    )
```

time: 93.2 us -> 49.2 us (0.53)
  waiting for transfers between devices: 64.8 us -> 0 us
  Pallas kernels: 0 us -> 38.2 us
  between operations: 14.1 us -> 0.65 us
  matrix products: 11.4 us -> 0 us
  local copies, waits for them, and re-layouts: 2.68 us -> 10.1 us
    all_gather x2 -> x0, waiting for transfers between devices: 63.4 us -> none  [the longest x1 41.3 us: on_device(): lax.all_gather(column_block, 'col', axis=1, tiled=True)]
    pallas_call x0 -> x1, Pallas kernels: none -> 38.2 us  [on_device(): pl.pallas_call(functools.partial(kernel, n_row, n_col), out_shape=(jax.Sh...]
    dot_general x3 -> x0, matrix products: 11.4 us -> none  [the longest x1 4.06 us: on_device(): jnp.dot(factor, lax.all_gather(row_block, 'row', axis=0, tiled=True), pre...]
    unnamed x8 -> x13, local copies, waits for them, and re-layouts: 1.15 us -> 10.1 us
    dynamic_slice x2 -> x0, local copies, waits for them, and re-layouts: 1.53 us -> none  [the longest x1 0.8 us: on_device(): lower_tile = lax.dynamic_slice_in_dim(lower_full, col_start, col_share, 1)]
    unnamed x2 -> x0, waiting for transfers between devices: 1.38 us -> none
  transfers between devices with their start and end apart: 2 -> 0, of which waited for: 2 -> 0; matrix products, arithmetic and copies ran while one was open for 5% -> 0% of each run, Pallas kernels for 0% -> 0%
where the time goes in v1:
time: 49.2 us; the launch traced here: 48.9 us
  Pallas kernels  38.2 us (78%)
  local copies, waits for them, and re-layouts  10.1 us (21%)
  between operations  0.65 us (1%)
    pallas_call x1, Pallas kernels, on_device(): pl.pallas_call(functools.partial(kernel, n_row, n_col), out_shape=(jax.Sh...  38.2 us
    unnamed x13, local copies, waits for them, and re-layouts  10.1 us

profile of v1, /device:TPU:0, one launch (start us, length us, event | category | flops | bytes accessed | tf_op | source)
XLA Modules:
  0.0 48.9 jit_solution(6253373104934594487)
XLA Ops:
  0.6 0.0 copy-start
  0.6 1.9 %copy-done = f32[768,1024]{1,0:T(8,128)S(1)} copy-done((f32[768,1024]{1,0:T(8,128)S(1)}, f32[768,1024]{1,0:T(8,128)}, u32[]{:S(2)}) %copy-start) | copy-done | bytes 3145752
  2.5 0.0 copy-start.1
  2.5 1.6 %copy-done.1 = bf16[1024,1024]{1,0:T(8,128)(2,1)S(1)} copy-done((bf16[1024,1024]{1,0:T(8,128)(2,1)S(1)}, bf16[1024,1024]{1,0:T(8,128)(2,1)}, u32[]{:S(2)}) %copy-start.1) | copy-done | bytes 2097176
  4.1 0.0 copy-start.2
  4.1 1.6 %copy-done.2 = bf16[1024,1024]{1,0:T(8,128)(2,1)S(1)} copy-done((bf16[1024,1024]{1,0:T(8,128)(2,1)S(1)}, bf16[1024,1024]{1,0:T(8,128)(2,1)}, u32[]{:S(2)}) %copy-start.2) | copy-done | bytes 2097176
  5.7 0.0 copy-start.3
  5.7 1.0 %copy-done.3 = bf16[768,256]{1,0:T(8,128)(2,1)S(1)} copy-done((bf16[768,256]{1,0:T(8,128)(2,1)S(1)}, bf16[768,256]{1,0:T(8,128)(2,1)}, u32[]{:S(2)}) %copy-start.3) | copy-done | bytes 393240
  6.7 0.0 copy-start.4
  6.7 0.9 %copy-done.4 = bf16[128,1024]{1,0:T(8,128)(2,1)S(1)} copy-done((bf16[128,1024]{1,0:T(8,128)(2,1)S(1)}, bf16[128,1024]{1,0:T(8,128)(2,1)}, u32[]{:S(2)}) %copy-start.4) | copy-done | bytes 262168
  7.7 38.2 %shard_map.76 = (bf16[768,256]{1,0:T(8,128)(2,1)S(1)}, bf16[128,1024]{1,0:T(8,128)(2,1)S(1)}, f32[768,1024]{1,0:T(8,128)S(1)}) custom-call(f32[768,1024]{1,0:T(8,128)S(1)} %copy-done, bf16[768,256]{1,0:T(8,128)(2,1)S(1)} %copy-done.3, bf16[128,1024]{1,0:T(8,128)(2,1)S(1)} %copy-done.4, bf16[1024,1024]{1,0:T(8,128)(2,1)S(1)} %copy-done.1, ...), custom_call_target="tpu_custom_call" | custom-call | tf_op jit(solution)/shard_map/pallas_call | solution.py:257
  45.8 0.7 %copy.11 = bf16[768,256]{1,0:T(8,128)(2,1)} copy(bf16[768,256]{1,0:T(8,128)(2,1)S(1)} %get-tuple-element.6) | data formatting | bytes 786432
  46.6 0.7 %copy.12 = bf16[128,1024]{1,0:T(8,128)(2,1)} copy(bf16[128,1024]{1,0:T(8,128)(2,1)S(1)} %get-tuple-element.7) | data formatting | bytes 524288
  47.3 1.7 %copy.13 = f32[768,1024]{1,0:T(8,128)} copy(f32[768,1024]{1,0:T(8,128)S(1)} %get-tuple-element.8) | data formatting | bytes 6291456
Async XLA Ops:
  0.6 1.9 %copy-start = (f32[768,1024]{1,0:T(8,128)S(1)}, f32[768,1024]{1,0:T(8,128)}, u32[]{:S(2)}) copy-start(f32[768,1024]{1,0:T(8,128)} %trailing.1) | copy-start | bytes 9437188
  2.5 1.6 %copy-start.1 = (bf16[1024,1024]{1,0:T(8,128)(2,1)S(1)}, bf16[1024,1024]{1,0:T(8,128)(2,1)}, u32[]{:S(2)}) copy-start(bf16[1024,1024]{1,0:T(8,128)(2,1)} %lower_inv.1) | copy-start | bytes 6291460
  4.1 1.6 %copy-start.2 = (bf16[1024,1024]{1,0:T(8,128)(2,1)S(1)}, bf16[1024,1024]{1,0:T(8,128)(2,1)}, u32[]{:S(2)}) copy-start(bf16[1024,1024]{1,0:T(8,128)(2,1)} %upper_inv.1) | copy-start | bytes 6291460
  5.7 1.0 %copy-start.3 = (bf16[768,256]{1,0:T(8,128)(2,1)S(1)}, bf16[768,256]{1,0:T(8,128)(2,1)}, u32[]{:S(2)}) copy-start(bf16[768,256]{1,0:T(8,128)(2,1)} %column_block.1) | copy-start | bytes 1179652
  6.7 0.9 %copy-start.4 = (bf16[128,1024]{1,0:T(8,128)(2,1)S(1)}, bf16[128,1024]{1,0:T(8,128)(2,1)}, u32[]{:S(2)}) copy-start(bf16[128,1024]{1,0:T(8,128)(2,1)} %row_block.1) | copy-start | bytes 786436

commit v2 on v1

--- a/solution.py
+++ b/solution.py
@@ -282,7 +282,7 @@
         compiler_params=pltpu.CompilerParams(
             collective_id=0, has_side_effects=True, vmem_limit_bytes=32 << 20
         ),
-    )(trailing, column_block, row_block, lower_inv, upper_inv)
+    )(*(pltpu.with_memory_space_constraint(x, pltpu.HBM) for x in (trailing, column_block, row_block, lower_inv, upper_inv)))
 
 
 def solution(mesh):

time: 49.2 us -> 42.4 us (0.86)
  local copies, waits for them, and re-layouts: 10.1 us -> 3.11 us
    unnamed x13 -> x3, local copies, waits for them, and re-layouts: 10.1 us -> 3.11 us
where the time goes in v2:
time: 42.4 us; the launch traced here: 42.2 us
  Pallas kernels  38.5 us (91%)
  local copies, waits for them, and re-layouts  3.11 us (7%)
  between operations  0.64 us (2%)
    pallas_call x1, Pallas kernels, on_device(): pl.pallas_call(functools.partial(kernel, n_row, n_col), out_shape=(jax.Sh...  38.5 us
    unnamed x3, local copies, waits for them, and re-layouts  3.11 us

profile of v2, /device:TPU:0, one launch (start us, length us, event | category | flops | bytes accessed | tf_op | source)
XLA Modules:
  0.0 42.2 jit_solution(1485197913269092502)
XLA Ops:
  0.6 38.5 %shard_map.76 = (bf16[768,256]{1,0:T(8,128)(2,1)S(1)}, bf16[128,1024]{1,0:T(8,128)(2,1)S(1)}, f32[768,1024]{1,0:T(8,128)S(1)}) custom-call(f32[768,1024]{1,0:T(8,128)} %trailing.1, bf16[768,256]{1,0:T(8,128)(2,1)} %column_block.1, bf16[128,1024]{1,0:T(8,128)(2,1)} %row_block.1, bf16[1024,1024]{1,0:T(8,128)(2,1)} %lower_inv.1, bf16[1024,1024]{1,0:T(8,128)(2,1)} %upper_inv.1), custom_call_target="tpu_custom_call" | custom-call | tf_op jit(solution)/shard_map/pallas_call | solution.py:257
  39.1 0.7 %copy.11 = bf16[768,256]{1,0:T(8,128)(2,1)} copy(bf16[768,256]{1,0:T(8,128)(2,1)S(1)} %get-tuple-element.6) | data formatting | bytes 786432
  39.9 0.7 %copy.12 = bf16[128,1024]{1,0:T(8,128)(2,1)} copy(bf16[128,1024]{1,0:T(8,128)(2,1)S(1)} %get-tuple-element.7) | data formatting | bytes 524288
  40.6 1.7 %copy.13 = f32[768,1024]{1,0:T(8,128)} copy(f32[768,1024]{1,0:T(8,128)S(1)} %get-tuple-element.8) | data formatting | bytes 6291456

commit v3 on v2

v3 whole, which is shorter than its diff:
```python
import functools

import jax
import jax.numpy as jnp
from jax import lax
from jax.experimental import pallas as pl
from jax.experimental.pallas import tpu as pltpu
from jax.sharding import PartitionSpec as P

MESH = pl.DeviceIdType.MESH
BLOCK = 256
PARTS = (3, 3, 3, 2, 1)
ROW_CHUNKS = 4


def chunks_of(rows):
    unit = rows // sum(PARTS)
    starts = [sum(PARTS[:k]) * unit for k in range(len(PARTS))]
    return [(start, part * unit) for start, part in zip(starts, PARTS)]


def reach(size, chunk):
    each = (size - 1) // 2
    extra = 1 if size % 2 == 0 else 0
    return (each + extra, each) if chunk % 2 == 0 else (each, each + extra)


def kernel(
    n_row, n_col,
    trailing, column_block, row_block, lower_inv, upper_inv,
    lower_tile, lower_last, upper, updated,
    gathered, strips, linv, uinv, lower,
    local_sem, own_sem, col_send, col_recv, row_send, row_recv, sib_send, sib_recv,
):
    rows, share = column_block.shape
    depth, cols = row_block.shape
    order = lower_inv.shape[0]
    pieces = chunks_of(rows)
    wide = cols // ROW_CHUNKS
    row, col = lax.axis_index("row"), lax.axis_index("col")
    chips = n_row // 2
    half = chips // 2
    core = lax.rem(row, 2)

    def snake(place):
        return place + (place // half) * (chips + half - 1 - 2 * place)

    place = snake(row // 2)

    def chip_at(offset):
        return snake(lax.rem(place + chips + offset, chips))

    sibling = {"row": row + 1 - 2 * core}
    row_next = {"row": chip_at(1) * 2 + core}
    row_prev = {"row": chip_at(-1) * 2 + core}
    after = {"col": col + 1}
    before = {"col": col - 1}
    has_after = col < n_col - 1
    has_before = col > 0

    load_l = pltpu.make_async_copy(lower_inv, linv, local_sem.at[0])
    load_u = pltpu.make_async_copy(upper_inv, uinv, local_sem.at[1])
    load_t = pltpu.make_async_copy(trailing, updated, local_sem.at[2])
    mine_c = pltpu.make_async_copy(column_block, gathered.at[col], own_sem.at[0])
    my_rows = pl.ds(pl.multiple_of(row * depth, depth), depth)
    mine_r = pltpu.make_async_copy(row_block, strips.at[my_rows], own_sem.at[1])

    barrier = pltpu.get_barrier_semaphore()

    def greet(device):
        pl.semaphore_signal(barrier, inc=1, device_id=device, device_id_type=MESH)

    pl.when(has_after)(lambda: greet(after))
    pl.when(has_before)(lambda: greet(before))
    for device in (row_next, row_prev, sibling):
        greet(device)
    mine_c.start()
    mine_r.start()
    load_l.start()
    load_u.start()
    ahead = (2 * n_col - 3 - col) // (n_col - 1)
    behind = (n_col - 2 + col) // (n_col - 1)
    pl.semaphore_wait(barrier, 3 + ahead + behind)

    sent = []

    def send(src, dst, send_sem, recv_sem, device):
        copy = pltpu.make_async_remote_copy(
            src_ref=src, dst_ref=dst, send_sem=send_sem, recv_sem=recv_sem,
            device_id=device, device_id_type=MESH,
        )
        copy.start()
        sent.append(copy)

    def arrived(dst, sem):
        pltpu.make_async_copy(dst, dst, sem).wait()

    def col_slot(owner, chunk):
        return gathered.at[owner, pl.ds(*pieces[chunk])]

    def col_copy(way, step, chunk):
        owner = col + (1 - step if way == 0 else step - 1)
        slot = col_slot(owner, chunk)
        return pltpu.make_async_remote_copy(
            src_ref=column_block.at[pl.ds(*pieces[chunk])] if step == 1 else slot,
            dst_ref=slot,
            send_sem=col_send.at[way, step - 1, chunk],
            recv_sem=col_recv.at[way, step - 1, chunk],
            device_id=after if way == 0 else before,
            device_id_type=MESH,
        )

    def sends(way, step):
        if way == 0:
            return has_after if step == 1 else has_after & (col >= step - 1)
        return has_before if step == 1 else has_before & (col + step - 1 < n_col)

    def takes(way, step):
        return col >= step if way == 0 else col + step < n_col

    def col_own(way):
        @pl.when(sends(way, 1))
        def _():
            for chunk in range(len(pieces)):
                col_copy(way, 1, chunk).start()

    def col_event(step, chunk):
        for way in range(2):
            @pl.when(takes(way, step))
            def _():
                slot = col_slot(col - step if way == 0 else col + step, chunk)
                arrived(slot, col_recv.at[way, step - 1, chunk])

            if step < n_col - 1:
                @pl.when(sends(way, step + 1))
                def _():
                    col_copy(way, step + 1, chunk).start()

    def col_drain():
        for way in range(2):
            for step in range(1, n_col):
                @pl.when(sends(way, step))
                def _():
                    for chunk in range(len(pieces)):
                        col_copy(way, step, chunk).wait_send()

    def strip(offset, lane, chunk):
        owner = chip_at(offset) * 2 + lane
        start = pl.multiple_of(owner * depth, depth)
        return strips.at[pl.ds(start, depth), pl.ds(chunk * wide, wide)]

    def row_send_to(way, step, chunk, src):
        offset = (1 - step) if way == 0 else (step - 1)
        send(
            src, strip(offset, core, chunk),
            row_send.at[way, step - 1, chunk], row_recv.at[way, step - 1, chunk],
            row_next if way == 0 else row_prev,
        )

    def share_strip(offset, chunk, src):
        at = offset + half
        send(
            src, strip(offset, core, chunk),
            sib_send.at[at, chunk], sib_recv.at[at, chunk], sibling,
        )

    shared = [[] for _ in range(ROW_CHUNKS)]

    def row_own(chunk):
        src = row_block.at[:, pl.ds(chunk * wide, wide)]
        for way in range(2):
            if reach(chips, chunk)[way] >= 1:
                row_send_to(way, 1, chunk, src)
        share_strip(0, chunk, src)
        shared[chunk].append(0)

    def row_event(step, chunk):
        for way in range(2):
            limit = reach(chips, chunk)[way]
            if step <= limit:
                offset = -step if way == 0 else step
                slot = strip(offset, core, chunk)
                arrived(slot, row_recv.at[way, step - 1, chunk])
                if step < limit:
                    row_send_to(way, step + 1, chunk, slot)
                share_strip(offset, chunk, slot)
                shared[chunk].append(offset)

    def row_shared(chunk):
        for offset in shared[chunk]:
            arrived(strip(offset, 1 - core, chunk), sib_recv.at[offset + half, chunk])

    def make_upper(chunk):
        at = pl.ds(chunk * wide, wide)
        for i in range(order // BLOCK):
            end = (i + 1) * BLOCK
            upper[pl.ds(i * BLOCK, BLOCK), at] = jnp.dot(
                linv[pl.ds(i * BLOCK, BLOCK), pl.ds(0, end)],
                strips[pl.ds(0, end), at],
                preferred_element_type=jnp.float32,
            ).astype(jnp.bfloat16)

    def make_lower(chunk):
        at = pl.ds(*pieces[chunk])
        parts = [gathered[k, at] for k in range(n_col)]
        left = jnp.concatenate(parts, axis=1)
        for j in range(order // BLOCK):
            end = (j + 1) * BLOCK
            lower[at, pl.ds(j * BLOCK, BLOCK)] = jnp.dot(
                left[:, :end],
                uinv[pl.ds(0, end), pl.ds(j * BLOCK, BLOCK)],
                preferred_element_type=jnp.float32,
            ).astype(jnp.bfloat16)
        if share % 128 == 0:
            lower_tile[at] = lower[at, pl.ds(pl.multiple_of(col * share, share), share)]
        else:
            for k in range(n_col):
                @pl.when(col == k)
                def _():
                    lower_tile[at] = lower[at, pl.ds(k * share, share)]
        if chunk == len(pieces) - 1:
            lower_last[...] = lower[at]

    def subtract(chunk):
        at = pl.ds(*pieces[chunk])

        @pl.loop(0, cols // BLOCK)
        def _(j):
            across = pl.ds(pl.multiple_of(j * BLOCK, BLOCK), BLOCK)
            updated[at, across] -= jnp.dot(
                lower[at], upper[:, across], preferred_element_type=jnp.float32
            )

    col_own(0)
    col_own(1)
    for chunk in range(ROW_CHUNKS):
        row_own(chunk)
    load_t.start()
    row_depth = max(max(reach(chips, r)) for r in range(ROW_CHUNKS))
    last = len(pieces) - 1
    for chunk in range(max(len(pieces), ROW_CHUNKS)):
        if chunk < ROW_CHUNKS:
            row_event(1, chunk)
        if chunk <= last:
            col_event(1, chunk)
    for step in range(2, row_depth + 1):
        for chunk in range(ROW_CHUNKS):
            row_event(step, chunk)
    mine_c.wait()
    mine_r.wait()
    load_l.wait()
    load_u.wait()
    for chunk in range(ROW_CHUNKS):
        row_shared(chunk)
        make_upper(chunk)
    load_t.wait()
    for step in range(2, n_col - 1):
        for chunk in range(len(pieces)):
            col_event(step, chunk)
    for chunk in range(len(pieces)):
        col_event(n_col - 1, chunk)
        make_lower(chunk)
        if chunk < last:
            subtract(chunk)
    for copy in sent:
        copy.wait_send()
    col_drain()


def finish(lower_last, lower_done, upper, partial, lower_tile, upper_tile, updated, rest, sem):
    rows, cols = partial.shape
    depth = upper_tile.shape[0]
    start = pl.multiple_of(lax.axis_index("row") * depth, depth)
    pieces = chunks_of(rows)
    at = pl.ds(*pieces[-1])
    copies = [
        pltpu.make_async_copy(partial.at[pl.ds(*piece)], updated.at[pl.ds(*piece)], sem.at[k])
        for k, piece in enumerate(pieces[:-1])
    ]
    copies.append(pltpu.make_async_copy(lower_done, lower_tile, sem.at[len(pieces)]))
    copies.append(
        pltpu.make_async_copy(upper.at[pl.ds(start, depth)], upper_tile, sem.at[len(pieces) + 1])
    )
    for copy in copies:
        copy.start()
    for j in range(cols // BLOCK):
        across = pl.ds(j * BLOCK, BLOCK)
        rest[:, across] = partial[at, across] - jnp.dot(
            lower_last[...], upper[:, across], preferred_element_type=jnp.float32
        )
    tail = pltpu.make_async_copy(rest, updated.at[at], sem.at[len(pieces) - 1])
    tail.start()
    for copy in copies:
        copy.wait()
    tail.wait()


def on_device(n_row, n_col, trailing, column_block, row_block, lower_inv, upper_inv):
    rows, share = column_block.shape
    depth, cols = row_block.shape
    order = lower_inv.shape[0]
    chips = n_row // 2
    hops = chips // 2
    narrow = jnp.bfloat16
    hbm = pl.BlockSpec(memory_space=pltpu.HBM)
    inside = pl.BlockSpec(memory_space=pltpu.VMEM)
    dma = pltpu.SemaphoreType.DMA
    count = len(PARTS)
    last = chunks_of(rows)[-1][1]
    inputs = (trailing, column_block, row_block, lower_inv, upper_inv)
    tile = jax.ShapeDtypeStruct((rows, share), narrow)
    whole = jax.ShapeDtypeStruct((rows, cols), jnp.float32)
    lower_done, lower_last, upper, partial = pl.pallas_call(
        functools.partial(kernel, n_row, n_col),
        out_shape=(
            tile,
            jax.ShapeDtypeStruct((last, order), narrow),
            jax.ShapeDtypeStruct((order, cols), narrow),
            whole,
        ),
        in_specs=[hbm] * 5,
        out_specs=(inside,) * 4,
        scratch_shapes=[
            pltpu.VMEM((n_col, rows, share), narrow),
            pltpu.VMEM((order, cols), narrow),
            pltpu.VMEM((order, order), narrow),
            pltpu.VMEM((order, order), narrow),
            pltpu.VMEM((rows, order), narrow),
            dma((3,)),
            dma((2,)),
            dma((2, n_col - 1, count)),
            dma((2, n_col - 1, count)),
            dma((2, hops, ROW_CHUNKS)),
            dma((2, hops, ROW_CHUNKS)),
            dma((2 * hops + 1, ROW_CHUNKS)),
            dma((2 * hops + 1, ROW_CHUNKS)),
        ],
        compiler_params=pltpu.CompilerParams(
            collective_id=0, has_side_effects=True, vmem_limit_bytes=32 << 20
        ),
    )(*(pltpu.with_memory_space_constraint(x, pltpu.HBM) for x in inputs))
    return pl.pallas_call(
        finish,
        out_shape=(tile, jax.ShapeDtypeStruct((depth, cols), narrow), whole),
        in_specs=[inside] * 4,
        out_specs=(hbm,) * 3,
        scratch_shapes=[pltpu.VMEM((last, cols), jnp.float32), dma((count + 2,))],
        compiler_params=pltpu.CompilerParams(vmem_limit_bytes=16 << 20),
    )(lower_last, lower_done, upper, partial)


def solution(mesh):
    specs = P("row", "col")
    return jax.shard_map(
        functools.partial(on_device, mesh.shape["row"], mesh.shape["col"]),
        mesh=mesh,
        in_specs=(specs, specs, specs, P(), P()),
        out_specs=(specs,) * 3,
        check_vma=False,
    )
```

time: 42.4 us -> 37 us (0.87)
  local copies, waits for them, and re-layouts: 3.11 us -> 0 us
  Pallas kernels: 38.5 us -> 36.2 us
    unnamed x3 -> x0, local copies, waits for them, and re-layouts: 3.11 us -> none
    pallas_call x1 -> x2, Pallas kernels: 38.5 us -> 36.2 us  [the longest x1 34.2 us: on_device(): pl.pallas_call(functools.partial(kernel, n_row, n_col), out_shape=(tile,...]
where the time goes in v3:
time: 37 us; the launch traced here: 36.8 us
  Pallas kernels  36.2 us (98%)
  between operations  0.64 us (2%)
    pallas_call x1, Pallas kernels, on_device(): pl.pallas_call(functools.partial(kernel, n_row, n_col), out_shape=(tile,...  34.2 us
    pallas_call x1, Pallas kernels, on_device(): pl.pallas_call(finish, out_shape=(tile, jax.ShapeDtypeStruct((depth, cols...  1.93 us

profile of v3, /device:TPU:0, one launch (start us, length us, event | category | flops | bytes accessed | tf_op | source)
XLA Modules:
  0.0 36.8 jit_solution(12796102695950191735)
XLA Ops:
  0.6 34.2 %shard_map.76 = (bf16[768,256]{1,0:T(8,128)(2,1)S(1)}, bf16[64,1024]{1,0:T(8,128)(2,1)S(1)}, bf16[1024,1024]{1,0:T(8,128)(2,1)S(1)}, f32[768,1024]{1,0:T(8,128)S(1)}) custom-call(f32[768,1024]{1,0:T(8,128)} %trailing.1, bf16[768,256]{1,0:T(8,128)(2,1)} %column_block.1, bf16[128,1024]{1,0:T(8,128)(2,1)} %row_block.1, bf16[1024,1024]{1,0:T(8,128)(2,1)} %lower_inv.1, ...), custom_call_target="tpu_custom_call" | custom-call | tf_op jit(solution)/shard_map/pallas_call | solution.py:313
  34.9 1.9 %shard_map.77 = (bf16[768,256]{1,0:T(8,128)(2,1)}, bf16[128,1024]{1,0:T(8,128)(2,1)}, f32[768,1024]{1,0:T(8,128)}) custom-call(bf16[64,1024]{1,0:T(8,128)(2,1)S(1)} %get-tuple-element.7.lower_last, bf16[768,256]{1,0:T(8,128)(2,1)S(1)} %get-tuple-element.8.lower_done, bf16[1024,1024]{1,0:T(8,128)(2,1)S(1)} %get-tuple-element.9.upper, ...), custom_call_target="tpu_custom_call" | custom-call | tf_op jit(solution)/shard_map/pallas_call | solution.py:342

commit v4 on v3

--- a/solution.py
+++ b/solution.py
@@ -9,7 +9,7 @@
 
 MESH = pl.DeviceIdType.MESH
 BLOCK = 256
-PARTS = (3, 3, 3, 2, 1)
+PARTS = (2, 2, 2, 2, 2, 2)
 ROW_CHUNKS = 4
 
 
@@ -30,7 +30,7 @@
     trailing, column_block, row_block, lower_inv, upper_inv,
     lower_tile, lower_last, upper, updated,
     gathered, strips, linv, uinv, lower,
-    local_sem, own_sem, col_send, col_recv, row_send, row_recv, sib_send, sib_recv,
+    local_sem, own_sem, col_send, col_recv, row_send, row_recv, sib_send, sib_recv, met,
 ):
     rows, share = column_block.shape
     depth, cols = row_block.shape
@@ -72,15 +72,21 @@
 
     pl.when(has_after)(lambda: greet(after))
     pl.when(has_before)(lambda: greet(before))
-    for device in (row_next, row_prev, sibling):
-        greet(device)
+    greet(row_next)
+    greet(row_prev)
+    pl.when(core == 0)(lambda: greet(sibling))
     mine_c.start()
     mine_r.start()
     load_l.start()
     load_u.start()
     ahead = (2 * n_col - 3 - col) // (n_col - 1)
     behind = (n_col - 2 + col) // (n_col - 1)
-    pl.semaphore_wait(barrier, 3 + ahead + behind)
+    pl.semaphore_wait(barrier, 2 + core + ahead + behind)
+
+    @pl.when(core == 1)
+    def _():
+        pl.semaphore_signal(met, inc=1, device_id=sibling, device_id_type=MESH)
+
 
     sent = []
 
@@ -171,8 +177,6 @@
         for way in range(2):
             if reach(chips, chunk)[way] >= 1:
                 row_send_to(way, 1, chunk, src)
-        share_strip(0, chunk, src)
-        shared[chunk].append(0)
 
     def row_event(step, chunk):
         for way in range(2):
@@ -236,6 +240,10 @@
     for chunk in range(ROW_CHUNKS):
         row_own(chunk)
     load_t.start()
+    pl.when(core == 0)(lambda: pl.semaphore_wait(met, 1))
+    for chunk in range(ROW_CHUNKS):
+        share_strip(0, chunk, row_block.at[:, pl.ds(chunk * wide, wide)])
+        shared[chunk].append(0)
     row_depth = max(max(reach(chips, r)) for r in range(ROW_CHUNKS))
     last = len(pieces) - 1
     for chunk in range(max(len(pieces), ROW_CHUNKS)):
@@ -334,6 +342,7 @@
             dma((2, hops, ROW_CHUNKS)),
             dma((2 * hops + 1, ROW_CHUNKS)),
             dma((2 * hops + 1, ROW_CHUNKS)),
+            pltpu.SemaphoreType.REGULAR,
         ],
         compiler_params=pltpu.CompilerParams(
             collective_id=0, has_side_effects=True, vmem_limit_bytes=32 << 20

time: 37 us -> 36.2 us (0.978)
  Pallas kernels: 36.2 us -> 35.4 us
    pallas_call x1, Pallas kernels: 34.2 us -> 33.5 us  [on_device(): pl.pallas_call(functools.partial(kernel, n_row, n_col), out_shape=(tile,...]
where the time goes in v4:
time: 36.2 us; the launch traced here: 36.1 us
  Pallas kernels  35.4 us (98%)
  between operations  0.64 us (2%)
    pallas_call x1, Pallas kernels, on_device(): pl.pallas_call(functools.partial(kernel, n_row, n_col), out_shape=(tile,...  33.5 us
    pallas_call x1, Pallas kernels, on_device(): pl.pallas_call(finish, out_shape=(tile, jax.ShapeDtypeStruct((depth, cols...  1.94 us

profile of v4, /device:TPU:0, one launch (start us, length us, event | category | flops | bytes accessed | tf_op | source)
XLA Modules:
  0.0 36.1 jit_solution(9965720023247799351)
XLA Ops:
  0.6 33.5 %shard_map.76 = (bf16[768,256]{1,0:T(8,128)(2,1)S(1)}, bf16[128,1024]{1,0:T(8,128)(2,1)S(1)}, bf16[1024,1024]{1,0:T(8,128)(2,1)S(1)}, f32[768,1024]{1,0:T(8,128)S(1)}) custom-call(f32[768,1024]{1,0:T(8,128)} %trailing.1, bf16[768,256]{1,0:T(8,128)(2,1)} %column_block.1, bf16[128,1024]{1,0:T(8,128)(2,1)} %row_block.1, bf16[1024,1024]{1,0:T(8,128)(2,1)} %lower_inv.1, ...), custom_call_target="tpu_custom_call" | custom-call | tf_op jit(solution)/shard_map/pallas_call | solution.py:321
  34.1 1.9 %shard_map.77 = (bf16[768,256]{1,0:T(8,128)(2,1)}, bf16[128,1024]{1,0:T(8,128)(2,1)}, f32[768,1024]{1,0:T(8,128)}) custom-call(bf16[128,1024]{1,0:T(8,128)(2,1)S(1)} %get-tuple-element.7.lower_last, bf16[768,256]{1,0:T(8,128)(2,1)S(1)} %get-tuple-element.8.lower_done, bf16[1024,1024]{1,0:T(8,128)(2,1)S(1)} %get-tuple-element.9.upper, ...), custom_call_target="tpu_custom_call" | custom-call | tf_op jit(solution)/shard_map/pallas_call | solution.py:351

commit v5 on v4

--- a/solution.py
+++ b/solution.py
@@ -9,7 +9,8 @@
 
 MESH = pl.DeviceIdType.MESH
 BLOCK = 256
-PARTS = (2, 2, 2, 2, 2, 2)
+TILE = 1024
+PARTS = (3, 3, 3, 3)
 ROW_CHUNKS = 4
 
 
@@ -228,9 +229,9 @@
     def subtract(chunk):
         at = pl.ds(*pieces[chunk])
 
-        @pl.loop(0, cols // BLOCK)
+        @pl.loop(0, cols // TILE)
         def _(j):
-            across = pl.ds(pl.multiple_of(j * BLOCK, BLOCK), BLOCK)
+            across = pl.ds(pl.multiple_of(j * TILE, TILE), TILE)
             updated[at, across] -= jnp.dot(
                 lower[at], upper[:, across], preferred_element_type=jnp.float32
             )

time: 36.2 us -> 35.1 us (0.970)
  Pallas kernels: 35.4 us -> 34.3 us
    pallas_call x1, Pallas kernels: 33.5 us -> 32.4 us  [on_device(): pl.pallas_call(functools.partial(kernel, n_row, n_col), out_shape=(tile,...]
where the time goes in v5:
time: 35.1 us; the launch traced here: 34.9 us
  Pallas kernels  34.3 us (98%)
  between operations  0.64 us (2%)
    pallas_call x1, Pallas kernels, on_device(): pl.pallas_call(functools.partial(kernel, n_row, n_col), out_shape=(tile,...  32.4 us
    pallas_call x1, Pallas kernels, on_device(): pl.pallas_call(finish, out_shape=(tile, jax.ShapeDtypeStruct((depth, cols...  1.93 us

profile of v5, /device:TPU:0, one launch (start us, length us, event | category | flops | bytes accessed | tf_op | source)
XLA Modules:
  0.0 34.9 jit_solution(16968531406417479039)
XLA Ops:
  0.6 32.4 %shard_map.76 = (bf16[768,256]{1,0:T(8,128)(2,1)S(1)}, bf16[192,1024]{1,0:T(8,128)(2,1)S(1)}, bf16[1024,1024]{1,0:T(8,128)(2,1)S(1)}, f32[768,1024]{1,0:T(8,128)S(1)}) custom-call(f32[768,1024]{1,0:T(8,128)} %trailing.1, bf16[768,256]{1,0:T(8,128)(2,1)} %column_block.1, bf16[128,1024]{1,0:T(8,128)(2,1)} %row_block.1, bf16[1024,1024]{1,0:T(8,128)(2,1)} %lower_inv.1, ...), custom_call_target="tpu_custom_call" | custom-call | tf_op jit(solution)/shard_map/pallas_call | solution.py:322
  33.0 1.9 %shard_map.77 = (bf16[768,256]{1,0:T(8,128)(2,1)}, bf16[128,1024]{1,0:T(8,128)(2,1)}, f32[768,1024]{1,0:T(8,128)}) custom-call(bf16[192,1024]{1,0:T(8,128)(2,1)S(1)} %get-tuple-element.7.lower_last, bf16[768,256]{1,0:T(8,128)(2,1)S(1)} %get-tuple-element.8.lower_done, bf16[1024,1024]{1,0:T(8,128)(2,1)S(1)} %get-tuple-element.9.upper, ...), custom_call_target="tpu_custom_call" | custom-call | tf_op jit(solution)/shard_map/pallas_call | solution.py:352

commit v6 on v5

--- a/solution.py
+++ b/solution.py
@@ -9,7 +9,6 @@
 
 MESH = pl.DeviceIdType.MESH
 BLOCK = 256
-TILE = 1024
 PARTS = (3, 3, 3, 3)
 ROW_CHUNKS = 4
 
@@ -228,13 +227,7 @@
 
     def subtract(chunk):
         at = pl.ds(*pieces[chunk])
-
-        @pl.loop(0, cols // TILE)
-        def _(j):
-            across = pl.ds(pl.multiple_of(j * TILE, TILE), TILE)
-            updated[at, across] -= jnp.dot(
-                lower[at], upper[:, across], preferred_element_type=jnp.float32
-            )
+        updated[at] -= jnp.dot(lower[at], upper[...], preferred_element_type=jnp.float32)
 
     col_own(0)
     col_own(1)
@@ -268,12 +261,13 @@
             col_event(step, chunk)
     for chunk in range(len(pieces)):
         col_event(n_col - 1, chunk)
+        if chunk == last:
+            for copy in sent:
+                copy.wait_send()
+            col_drain()
         make_lower(chunk)
         if chunk < last:
             subtract(chunk)
-    for copy in sent:
-        copy.wait_send()
-    col_drain()
 
 
 def finish(lower_last, lower_done, upper, partial, lower_tile, upper_tile, updated, rest, sem):

time: 35.1 us -> 35.1 us (level)
  no operation moved by 1% of the time
where the time goes in v6:
time: 35.1 us; the launch traced here: 34.9 us
  Pallas kernels  34.3 us (98%)
  between operations  0.64 us (2%)
    pallas_call x1, Pallas kernels, on_device(): pl.pallas_call(functools.partial(kernel, n_row, n_col), out_shape=(tile,...  32.3 us
    pallas_call x1, Pallas kernels, on_device(): pl.pallas_call(finish, out_shape=(tile, jax.ShapeDtypeStruct((depth, cols...  1.93 us

profile of v6, /device:TPU:0, one launch (start us, length us, event | category | flops | bytes accessed | tf_op | source)
XLA Modules:
  0.0 34.9 jit_solution(4917100766334955458)
XLA Ops:
  0.6 32.3 %shard_map.76 = (bf16[768,256]{1,0:T(8,128)(2,1)S(1)}, bf16[192,1024]{1,0:T(8,128)(2,1)S(1)}, bf16[1024,1024]{1,0:T(8,128)(2,1)S(1)}, f32[768,1024]{1,0:T(8,128)S(1)}) custom-call(f32[768,1024]{1,0:T(8,128)} %trailing.1, bf16[768,256]{1,0:T(8,128)(2,1)} %column_block.1, bf16[128,1024]{1,0:T(8,128)(2,1)} %row_block.1, bf16[1024,1024]{1,0:T(8,128)(2,1)} %lower_inv.1, ...), custom_call_target="tpu_custom_call" | custom-call | tf_op jit(solution)/shard_map/pallas_call | solution.py:316
  33.0 1.9 %shard_map.77 = (bf16[768,256]{1,0:T(8,128)(2,1)}, bf16[128,1024]{1,0:T(8,128)(2,1)}, f32[768,1024]{1,0:T(8,128)}) custom-call(bf16[192,1024]{1,0:T(8,128)(2,1)S(1)} %get-tuple-element.7.lower_last, bf16[768,256]{1,0:T(8,128)(2,1)S(1)} %get-tuple-element.8.lower_done, bf16[1024,1024]{1,0:T(8,128)(2,1)S(1)} %get-tuple-element.9.upper, ...), custom_call_target="tpu_custom_call" | custom-call | tf_op jit(solution)/shard_map/pallas_call | solution.py:346
